TPU v7x, 128 devices: a whole 4x4x4 slice. The times are simulated.
128 devices in a mesh: vae: 8 (over x_hi, z), seq: 16 (over x_lo, y, core).
Axes of the slice: x: 4 (x_hi: 2, x_lo: 2; x = x_hi * 2 + x_lo), y: 4, z: 4, core: 2. Of those that a mesh axis runs over, the one named last changes fastest.
Arguments:
- video: float32 [32, 256, 512], P('vae', 'seq')
- frame_counts: int32 [8], replicated, may hold values from 2 to 4, as said below
- conv_weight: float32 [3, 512, 512], replicated, may hold values from -0.15625 to 0.15625
- conv_bias: float32 [512], replicated, may hold values from -4 to 4
- norm_gain: float32 [512], replicated, may hold values from 0.1 to 1.9
- norm_bias: float32 [512], replicated, may hold values from -3 to 3
- embed_weight: bfloat16 [512, 3072], replicated, may hold values from -0.25 to 0.25
- embed_bias: float32 [3072], replicated, may hold values from -3 to 3
- shift: float32 [3072], replicated, may hold values from -3 to 3
- scale: float32 [3072], replicated, may hold values from -3 to 3
- gate: float32 [3072], replicated, may hold values from 1 to 3
- qkv_weight: bfloat16 [3072, 3, 3072], P(None, None, 'vae')
- q_gain: float32 [128], replicated, may hold values from 1 to 6
- k_gain: float32 [128], replicated, may hold values from 1 to 6
- out_weight: bfloat16 [3072, 3072], P('vae'), may hold values from -0.109375 to 0.109375
Outputs:
- result: bfloat16 [32, 256, 3072], P(None, 'seq', 'vae')
Inputs may be any that keep to these rules, and one draw needn't show every extreme that they name: `frame_counts`: every index of vae has at least 2 live slots; at least one has all 4 live.
All inputs are finite; a program needn't handle non-finite values.
Results may differ from a plain program's by a relative error of at most 0.013.
The roundings to bfloat16 on the way count: a program that leaves them out, or rounds other values in their place, can miss the bound.
Values may be sent and summed in bfloat16 or wider, within the bound.
A program may use at most 192 MiB of HBM per device.

v0:
```python
import math

import jax
import jax.numpy as jnp
from jax import lax
from jax.sharding import PartitionSpec as P

GROUPS = 32
HD = 128


def from_behind(x, axis, by):
    count = lax.axis_size(axis)
    pairs = [(i, i + by) for i in range(count) if 0 <= i + by < count]
    return lax.ppermute(x, axis, pairs)


def head_norm(values, weights):
    return values * lax.rsqrt(jnp.mean(values * values, axis=-1, keepdims=True) + 1e-06) * weights


def body(
    video,
    frame_counts,
    conv_weight,
    conv_bias,
    norm_gain,
    norm_bias,
    embed_weight,
    embed_bias,
    shift,
    scale,
    gate,
    qkv_weight,
    q_gain,
    k_gain,
    out_weight,
):
    highest = lax.Precision.HIGHEST
    fdev, pdev, chans = video.shape
    nvae = lax.axis_size("vae")
    nseq = lax.axis_size("seq")
    me_vae = lax.axis_index("vae")
    mine = frame_counts[me_vae]
    tail = lax.dynamic_slice_in_dim(video, mine - 2, 2, 0)
    prior = from_behind(tail, "vae", 1)
    extended = jnp.concatenate([prior, video], 0)
    conv = conv_bias + jnp.zeros((fdev, pdev, chans), jnp.float32)
    for tap in range(3):
        conv = conv + jnp.einsum(
            "fpc,cd->fpd", extended[2 - tap : 2 - tap + fdev], conv_weight[tap], precision=highest
        )
    local_live = (jnp.arange(fdev) < mine).astype(jnp.float32)[:, None, None]
    masked = conv * local_live
    width = chans // GROUPS
    first = masked.reshape(fdev, pdev, GROUPS, width).sum((0, 1, 3))
    second = (masked * conv).reshape(fdev, pdev, GROUPS, width).sum((0, 1, 3))
    first, second = lax.psum((first, second), ("vae", "seq"))
    number = jnp.sum(frame_counts).astype(jnp.float32) * (pdev * nseq * width)
    mean = first / number
    var = second / number - mean * mean
    centre = jnp.repeat(mean, width)
    inverse = jnp.repeat(lax.rsqrt(var + 1e-06), width)
    act = jax.nn.silu((conv - centre) * inverse * norm_gain + norm_bias).astype(jnp.bfloat16)
    frames_total = fdev * nvae
    slot_live = (jnp.arange(frames_total) % fdev < jnp.repeat(frame_counts, fdev)).astype(
        jnp.float32
    )
    count_frames = act.shape[0]
    projected = (
        jnp.dot(act.reshape(-1, chans), embed_weight, preferred_element_type=jnp.float32)
        + embed_bias
    )
    alive = lax.dynamic_slice_in_dim(slot_live, me_vae * fdev, count_frames, 0)
    own_tokens = (projected.reshape(count_frames, pdev, -1) * alive[:, None, None]).astype(
        jnp.bfloat16
    )
    tokens = lax.all_gather(own_tokens, "vae", axis=0, tiled=True)
    nloc = frames_total * pdev
    dwidth = tokens.shape[2]
    rows = tokens.reshape(nloc, dwidth).astype(jnp.float32)
    centred = rows - jnp.mean(rows, axis=-1, keepdims=True)
    spread = jnp.mean(centred * centred, axis=-1, keepdims=True)
    hidden = (centred * lax.rsqrt(spread + 1e-06) * (1.0 + scale) + shift).astype(jnp.bfloat16)
    proj = jnp.dot(hidden, qkv_weight.reshape(dwidth, -1), preferred_element_type=jnp.float32)
    inner = qkv_weight.shape[2]
    heads = inner // HD
    queries = head_norm(proj[:, :inner].reshape(nloc, heads, HD), q_gain).astype(jnp.bfloat16)
    keys = head_norm(proj[:, inner : 2 * inner].reshape(nloc, heads, HD), k_gain).astype(
        jnp.bfloat16
    )
    values = proj[:, 2 * inner :].reshape(nloc, heads, HD).astype(jnp.bfloat16)
    key_live = jnp.repeat(slot_live, pdev)
    root = math.sqrt(HD)
    best = jnp.full((heads, nloc), -1e30, jnp.float32)
    key_piece = lax.all_gather(keys, "seq", axis=0, tiled=True)
    value_piece = lax.all_gather(values, "seq", axis=0, tiled=True)
    length = key_piece.shape[0]
    alive = jnp.take(key_live, jnp.arange(length) % nloc) > 0.5
    scores = (
        jnp.einsum("nhd,khd->hnk", queries, key_piece, preferred_element_type=jnp.float32) / root
    )
    scores = jnp.where(alive[None, None, :], scores, -1e30)
    top = jnp.maximum(best, jnp.max(scores, axis=-1))
    weights = jnp.where(alive[None, None, :], jnp.exp(scores - top[..., None]), 0.0)
    summed = jnp.sum(weights, axis=-1)
    accum = jnp.einsum(
        "hnk,khd->nhd",
        weights.astype(jnp.bfloat16),
        value_piece,
        preferred_element_type=jnp.float32,
    )
    best, summed, accum = (top, summed, accum)
    attended = accum / jnp.transpose(summed, (1, 0))[..., None]
    merged = attended.reshape(nloc, inner).astype(jnp.bfloat16)
    partial_out = jnp.dot(merged, out_weight, preferred_element_type=jnp.float32)
    mixed = lax.psum_scatter(partial_out, "vae", scatter_dimension=1, tiled=True)
    columns = mixed.shape[1]
    residual = lax.dynamic_slice_in_dim(rows, me_vae * columns, columns, 1)
    gate_part = lax.dynamic_slice_in_dim(gate, me_vae * columns, columns, 0)
    result = ((residual + gate_part * mixed) * key_live[:, None]).astype(jnp.bfloat16)
    return result.reshape(frames_total, pdev, columns)


def solution(mesh):
    in_specs = (
        P("vae", "seq", None),
        P(),
        P(),
        P(),
        P(),
        P(),
        P(),
        P(),
        P(),
        P(),
        P(),
        P(None, None, "vae"),
        P(),
        P(),
        P("vae", None),
    )
    out_specs = P(None, "seq", "vae")
    return jax.shard_map(body, mesh=mesh, in_specs=in_specs, out_specs=out_specs, check_vma=False)
```

profile of v0, /device:TPU:0, one launch (start us, length us, event | category | flops | bytes accessed | tf_op | source)
XLA Modules:
  0.0 400.2 jit_solution(12064693817004700212)
XLA Ops:
  6.5 1.4 dynamic_slice.15
  10.1 3.9 collective-permute-start
  14.0 1.4 reduce_sum.89
  16.9 2.0 convolution_add_fusion.1
  20.5 2.0 fusion.10
  22.5 2.0 fusion.22
  24.9 65.9 %all-reduce = (f32[32]{0:T(128)S(1)}, f32[32]{0:T(128)S(1)}) all-reduce(f32[32]{0:T(128)S(1)} %reduce_sum.88, f32[32]{0:T(128)S(1)} %reduce_sum.92), channel_id=1, replica_groups=mesh['vae'=8,'seq'=16] {'vae','seq'}, use_global_device_ids=true, to_apply=%region_2.0 | all-reduce | flops 64 | bytes 512 | tf_op jit(solution)/shard_map/psum | solution.py:58
  91.9 1.4 convolution_add_fusion
  94.2 10.3 %copy.25 = bf16[3072,3,384]{0,2,1:T(8,128)(2,1)} copy(bf16[3072,3,384]{2,0,1:T(8,128)(2,1)} %param.26) | data formatting | bytes 14155776 | tf_op args[11]
  104.6 49.5 %all-gather.4.cloned.1.call-done = bf16[32,16,3072]{2,1,0:T(8,128)(2,1)} async-done(((bf16[4,16,3072]{2,1,0:T(8,128)(2,1)}), bf16[32,16,3072]{2,1,0:T(8,128)(2,1)}) %all-gather.4.cloned.1.call-update) | async-done | bytes 3145744 | tf_op jit(solution)/shard_map/all_gather | solution.py:78
  154.0 2.5 convert_reduce_fusion
  156.6 3.6 multiply_reduce_fusion
  160.2 1.7 add_convert_fusion
  161.9 4.3 %fusion.33 = f32[512,1152]{1,0:T(8,128)S(1)} fusion(bf16[512,3072]{1,0:T(8,128)(2,1)S(1)} %bitcast.49, bf16[3072,1152]{0,1:T(8,128)(2,1)S(1)} %bitcast.46), kind=kOutput, calls=%fused_computation.71 | convolution fusion | flops 3623878656 | bytes 12582912 | tf_op jit(solution)/shard_map/dot_general | solution.py:85
  166.3 1.3 copy-done.5
  169.4 1.2 slice.51
  172.0 51.2 %gather_fusion = f32[8192]{0:T(1024)S(1)} fusion(f32[512]{0:T(512)S(1)} %reshape.176, s32[8192]{0:T(1024)S(1)} %broadcast_clamp_fusion), kind=kCustom, calls=%fused_computation | custom fusion | bytes 98304 | tf_op jit(solution)/shard_map/jit(_take)/gather | solution.py:99
  223.6 21.7 %fusion = (f32[3,512]{1,0:T(4,128)S(1)}, f32[3,512,8192]{2,1,0:T(8,128)}) fusion(pred[8192]{0:T(1024)(128)(4,1)S(1)} %select_compare_fusion, bf16[8192,3,128]{2,0,1:T(8,128)(2,1)} %all-gather.8.cloned.1.call-done, f32[512,3,128]{0,2,1:T(8,128)S(1)} %bitcast.45, f32[128]{0:T(128)S(1)} %copy-done.6, f32[512,3]{0,1:T(4,128)S(1)} %add_rsqrt_fusion.2), kind=kOutput, calls=%fused_computation.3 | convolution fusion | flops 3259562496 | bytes 57430528 | tf_op jit(solution)/shard_map/nhd,khd->hnk/dot_general | solution.py:101
  245.3 23.2 %fusion.1 = f32[3,512]{1,0:T(4,128)S(1)} fusion(f32[3,512,8192]{2,1,0:T(8,128)} %get-tuple-element.15, f32[3,512]{1,0:T(4,128)S(1)} %broadcast_maximum_fusion, pred[8192]{0:T(1024)(128)(4,1)S(1)} %select_compare_fusion), kind=kLoop, calls=%fused_computation.4 | loop fusion | flops 62913024 | bytes 50352128 | tf_op jit(solution)/shard_map/reduce_sum | solution.py:106
  268.5 22.0 %divide_convert_fusion = bf16[512,3,128]{0,2,1:T(8,128)(2,1)S(1)} fusion(bf16[8192,3,128]{0,2,1:T(8,128)(2,1)} %all-gather.6.cloned.1.call-done, f32[3,512,8192]{2,1,0:T(8,128)} %get-tuple-element.15, f32[3,512]{1,0:T(4,128)S(1)} %broadcast_maximum_fusion, pred[8192]{0:T(1024)(128)(4,1)S(1)} %select_compare_fusion, f32[512,3]{0,1:T(4,128)S(1)} %bitcast.55), kind=kOutput, calls=%fused_computation.25 | convolution fusion | flops 3284533248 | bytes 57036800 | tf_op jit(solution)/shard_map/hnk,khd->nhd/dot_general | solution.py:107
  290.6 4.5 %fusion.34 = f32[512,3072]{1,0:T(8,128)} fusion(bf16[512,384]{0,1:T(8,128)(2,1)S(1)} %bitcast.52, bf16[384,3072]{1,0:T(8,128)(2,1)S(1)} %copy-done.4), kind=kOutput, calls=%fused_computation.72 | convolution fusion | flops 1207959552 | bytes 9043968 | tf_op jit(solution)/shard_map/dot_general | solution.py:116
  296.0 5.4 %bitcast_convert_fusion = f32[512,3072]{1,0:T(8,128)} fusion(bf16[32,16,3072]{2,1,0:T(8,128)(2,1)} %all-gather.4.cloned.1.call-done), kind=kLoop, calls=%fused_computation.70 | loop fusion | flops 1572864 | bytes 9437184 | tf_op jit(solution)/shard_map/convert_element_type | solution.py:81
  301.4 90.0 %reduce-scatter.2.cloned.1.call-done = f32[512,384]{1,0:T(8,128)} async-done(((f32[512,3072]{1,0:T(8,128)}), f32[512,384]{1,0:T(8,128)}) %reduce-scatter.2.cloned.1.call-update) | async-done | bytes 786448 | tf_op jit(solution)/shard_map/reduce_scatter | solution.py:117
  391.4 2.3 multiply_convert_fusion
  (69 shorter events, 10.3 us)
Async XLA Ops:
  6.5 85.4 %copy-start = (bf16[512,3072]{1,0:T(8,128)(2,1)S(1)}, bf16[512,3072]{1,0:T(8,128)(2,1)}, u32[]{:S(2)}) copy-start(bf16[512,3072]{1,0:T(8,128)(2,1)} %param.21) | copy-start | bytes 9437188
  6.5 147.5 %all-gather.4.cloned.1.call-start = ((), (), s32[]{:S(2)}) async-start(), calls=%async_computation.1 | async-start | bytes 3538944 | tf_op jit(solution)/shard_map/all_gather | solution.py:78
  10.1 9.5 %collective-permute-start = (f32[2,16,512]{2,1,0:T(8,128)S(1)}, f32[2,16,512]{2,1,0:T(8,128)S(1)}, u32[]{:S(2)}, u32[]{:S(2)}) collective-permute-start(f32[2,16,512]{2,1,0:T(8,128)S(1)} %constant_dynamic-slice_fusion), channel_id=1, source_target_pairs={{0,16},{16,32},{32,48},{48,64},{64,80},{80,96},{96,112},{1,17},{17... | collective-permute-start | bytes 196616 | tf_op jit(solution)/shard_map/ppermute | solution.py:15
  94.2 10.4 %copy-start.8 = (f32[3072]{0:T(1024)S(1)}, f32[3072]{0:T(1024)}, u32[]{:S(2)}) copy-start(f32[3072]{0:T(1024)} %param.24) | copy-start | bytes 36868
  94.2 129.4 %all-gather.8.cloned.1.call-start = ((), (), s32[]{:S(2)}) async-start(), calls=%async_computation.3 | async-start | bytes 6684672 | tf_op jit(solution)/shard_map/all_gather | solution.py:96
  104.5 55.6 %copy-start.7 = (f32[3072]{0:T(1024)S(1)}, f32[3072]{0:T(1024)}, u32[]{:S(2)}) copy-start(f32[3072]{0:T(1024)} %param.23) | copy-start | bytes 36868
  154.0 6.2 %copy-start.2 = (bf16[32,16,3072]{2,1,0:T(8,128)(2,1)S(1)}, bf16[32,16,3072]{2,1,0:T(8,128)(2,1)}, u32[]{:S(2)}) copy-start(bf16[32,16,3072]{2,1,0:T(8,128)(2,1)} %all-gather.4.cloned.1.call-done) | copy-start | bytes 9437188
  154.0 7.9 %copy-start.3 = (bf16[3072,3,384]{0,2,1:T(8,128)(2,1)S(1)}, bf16[3072,3,384]{0,2,1:T(8,128)(2,1)}, u32[]{:S(2)}) copy-start(bf16[3072,3,384]{0,2,1:T(8,128)(2,1)} %copy.25) | copy-start | bytes 21233668
  166.2 1.4 copy-start.5
  166.2 2.1 copy-start.9
  169.3 99.2 %all-gather.6.cloned.1.call-start = ((), (), s32[]{:S(2)}) async-start(), calls=%async_computation.2 | async-start | bytes 6684672 | tf_op jit(solution)/shard_map/all_gather | solution.py:97
  171.5 219.9 %reduce-scatter.2.cloned.1.call-start = ((), (), s32[]{:S(2)}) async-start(), calls=%async_computation.4 | async-start | bytes 7077888 | tf_op jit(solution)/shard_map/reduce_scatter | solution.py:117
  171.9 51.7 %copy-start.6 = (f32[128]{0:T(128)S(1)}, f32[128]{0:T(128)}, u32[]{:S(2)}) copy-start(f32[128]{0:T(128)} %param.27) | copy-start | bytes 1540
  268.5 22.0 %copy-start.4 = (bf16[384,3072]{1,0:T(8,128)(2,1)S(1)}, bf16[384,3072]{1,0:T(8,128)(2,1)}, u32[]{:S(2)}) copy-start(bf16[384,3072]{1,0:T(8,128)(2,1)} %param.29) | copy-start | bytes 7077892
  295.1 98.6 %copy-start.1 = (bf16[512,3072]{1,0:T(8,128)(2,1)S(1)}, bf16[512,3072]{1,0:T(8,128)(2,1)}, u32[]{:S(2)}) copy-start(bf16[512,3072]{1,0:T(8,128)(2,1)} %param.21) | copy-start | bytes 9437188
Sparse Core Ops, SparseCore 0:
  94.3 59.7 all-gather.3
  169.4 40.0 all-gather.7
  211.2 43.1 all-gather.5
  295.2 96.1 reduce-scatter.1
where the time goes:
time: 401 us; the launch traced here: 400 us
  waiting for transfers between devices  140 us (35%)
  local copies, waits for them, and re-layouts  71.5 us (18%)
  blocking collectives  65.9 us (16%)
  matrix products  59.8 us (15%)
  other arithmetic  43.8 us (11%)
  between operations  15.4 us (4%)
  starting transfers between devices  4.23 us (1%)
    reduce_scatter x1, waiting for transfers between devices, body(): lax.psum_scatter(partial_out, 'vae', scatter_dimension=1, tiled=True)  90 us
    psum x1, blocking collectives, body(): first, second = lax.psum((first, second), ('vae', 'seq'))  65.9 us
    gather x1, local copies, waits for them, and re-layouts, body(): alive = jnp.take(key_live, jnp.arange(length) % nloc) > 0.5  51.2 us
    all_gather x1, waiting for transfers between devices, body(): tokens = lax.all_gather(own_tokens, 'vae', axis=0, tiled=True)  49.5 us
    reduce_sum x1, other arithmetic, body(): summed = jnp.sum(weights, axis=-1)  23.2 us
    dot_general x1, matrix products, body(): jnp.einsum('hnk,khd->nhd', weights.astype(jnp.bfloat16), value_piece, pre...  22 us
    dot_general x1, matrix products, body(): jnp.einsum('nhd,khd->hnk', queries, key_piece, preferred_element_type=jnp...  21.7 us
    unnamed x22, local copies, waits for them, and re-layouts  11.7 us
  transfers between devices with their start and end apart: 5, of which 2 were waited for; matrix products, arithmetic and copies ran while one was open for 30% of the time, Pallas kernels for 0%

commit v1 on v0

v1 whole, which is shorter than its diff:
```python
import functools
import math

import jax
import jax.numpy as jnp
from jax import lax
from jax.experimental import pallas as pl
from jax.experimental.pallas import tpu as pltpu
from jax.sharding import PartitionSpec as P

GROUPS = 32
HD = 128
NV = 8
NS = 16
F32 = jnp.float32
BF16 = jnp.bfloat16
MESH = pl.DeviceIdType.MESH


def mod(a, n):
    return lax.rem(a + n, n)


def tokens_kernel(
    video, counts, conv_w, conv_b, norm_g, norm_b, embed_w, embed_b, shift, scale,
    hidden, resid,
    halo, w_hi, w_lo, sums_v, sums_s, act, tokens,
    halo_sem, ssem1, rsem1, ssem2, rsem2, asend, arecv,
):
    v = lax.axis_index("vae")
    s = lax.axis_index("seq")
    rows, chans = video.shape
    pdev = 16
    width = chans // GROUPS

    barrier = pltpu.get_barrier_semaphore()
    for d in range(1, NV):
        pl.semaphore_signal(barrier, inc=1, device_id=(mod(v + d, NV), s), device_id_type=MESH)
    for d in range(1, NS):
        pl.semaphore_signal(barrier, inc=1, device_id=(v, mod(s + d, NS)), device_id_type=MESH)

    @pl.when(v == 0)
    def _():
        halo[...] = jnp.zeros_like(halo)

    pl.semaphore_wait(barrier, NV - 1 + NS - 1)
    halo_copy = pltpu.make_async_remote_copy(
        src_ref=video, dst_ref=halo, send_sem=halo_sem.at[0], recv_sem=halo_sem.at[1],
        device_id=(mod(v + 1, NV), s), device_id_type=MESH,
    )

    @pl.when(v < NV - 1)
    def _():
        halo_copy.start()

    for tap in range(3):
        w = conv_w[tap]
        hi = w.astype(BF16)
        w_hi[tap] = hi
        w_lo[tap] = (w - hi.astype(F32)).astype(BF16)

    mine = counts[v]
    before = counts[jnp.maximum(v - 1, 0)]

    @pl.when(v > 0)
    def _():
        halo_copy.wait_recv()

    prior = jnp.where(
        before == 2, halo[0:32], jnp.where(before == 3, halo[16:48], halo[32:64])
    )
    ext = jnp.concatenate([prior, video[...]], 0)
    e_hi = ext.astype(BF16)
    e_lo = (ext - e_hi.astype(F32)).astype(BF16)
    both = jnp.zeros((2 * rows, chans), F32)
    low = jnp.zeros((rows, chans), F32)
    for tap in range(3):
        a = 32 - 16 * tap
        x_hi = e_hi[a : a + rows]
        both += jnp.dot(
            jnp.concatenate([x_hi, e_lo[a : a + rows]], 0), w_hi[tap], preferred_element_type=F32
        )
        low += jnp.dot(x_hi, w_lo[tap], preferred_element_type=F32)
    conv = both[:rows] + (both[rows:] + low) + conv_b[...]
    row_frame = lax.broadcasted_iota(jnp.int32, (rows, chans), 0) // pdev
    masked = jnp.where(row_frame < mine, conv, 0.0)
    first = jnp.sum(masked, axis=0, keepdims=True)
    second = jnp.sum(masked * conv, axis=0, keepdims=True)
    sums_v[v] = jnp.concatenate([first, second], 0)

    @pl.when(v < NV - 1)
    def _():
        halo_copy.wait_send()

    sends = []
    for d in range(1, NV):
        c = pltpu.make_async_remote_copy(
            src_ref=sums_v.at[v], dst_ref=sums_v.at[v], send_sem=ssem1.at[d], recv_sem=rsem1.at[d],
            device_id=(mod(v + d, NV), s), device_id_type=MESH,
        )
        c.start()
        sends.append(c)
    for c in sends:
        c.wait()
    total = sums_v[0]
    for u in range(1, NV):
        total += sums_v[u]
    sums_s[s] = total
    sends = []
    for d in range(1, NS):
        c = pltpu.make_async_remote_copy(
            src_ref=sums_s.at[s], dst_ref=sums_s.at[s], send_sem=ssem2.at[d], recv_sem=rsem2.at[d],
            device_id=(v, mod(s + d, NS)), device_id_type=MESH,
        )
        c.start()
        sends.append(c)
    gi = lax.broadcasted_iota(jnp.int32, (chans, chans), 0) // width
    gj = lax.broadcasted_iota(jnp.int32, (chans, chans), 1) // width
    same = jnp.where(gi == gj, 1.0, 0.0).astype(BF16)
    live = counts[0]
    for u in range(1, NV):
        live += counts[u]
    for c in sends:
        c.wait()
    total = sums_s[0]
    for u in range(1, NS):
        total += sums_s[u]
    p1 = total.astype(BF16)
    r1 = total - p1.astype(F32)
    p2 = r1.astype(BF16)
    p3 = (r1 - p2.astype(F32)).astype(BF16)
    grouped = (
        jnp.dot(p3, same, preferred_element_type=F32)
        + jnp.dot(p2, same, preferred_element_type=F32)
        + jnp.dot(p1, same, preferred_element_type=F32)
    )
    number = live.astype(F32) * (pdev * NS * width)
    mean = grouped[0:1] / number
    var = grouped[1:2] / number - mean * mean
    y = (conv - mean) * lax.rsqrt(var + 1e-06) * norm_g[...] + norm_b[...]
    act[v] = (y / (1.0 + jnp.exp(-y))).astype(BF16)

    far = mod(v + 4, NV)
    base = (v // 4) * 4
    fbase = 4 - base
    z = lax.rem(v, 4)
    up, down, opp = mod(z + 1, 4), mod(z - 1, 4), mod(z + 2, 4)
    half = rows // 2

    def hop(slot, lo, n, dev, sem_s, sem_r):
        ref = act.at[slot, pl.ds(lo, n)]
        return pltpu.make_async_remote_copy(
            src_ref=ref, dst_ref=ref, send_sem=asend.at[sem_s], recv_sem=arecv.at[sem_r],
            device_id=(dev, s), device_id_type=MESH,
        )

    far_c = hop(v, 0, rows, far, 0, 0)
    up_c = hop(v, 0, rows, base + up, 1, 1)
    dn_c = hop(v, 0, rows, base + down, 2, 2)
    far_c.start()
    up_c.start()
    dn_c.start()
    far_c.wait_recv()
    fup_c = hop(far, 0, rows, base + up, 3, 3)
    fdn_c = hop(far, 0, rows, base + down, 4, 4)
    fup_c.start()
    fdn_c.start()
    up_c.wait_recv()
    o1 = hop(base + down, 0, half, base + up, 5, 5)
    o1.start()
    dn_c.wait_recv()
    o2 = hop(base + up, half, half, base + down, 6, 6)
    o2.start()
    fup_c.wait_recv()
    o3 = hop(fbase + down, 0, half, base + up, 7, 7)
    o3.start()
    fdn_c.wait_recv()
    o4 = hop(fbase + up, half, half, base + down, 8, 8)
    o4.start()
    for c in (o1, o2, o3, o4):
        c.wait_recv()
    for c in (far_c, up_c, dn_c, fup_c, fdn_c, o1, o2, o3, o4):
        c.wait_send()

    total_rows = NV * rows
    dwidth = embed_w.shape[1]
    idx = lax.broadcasted_iota(jnp.int32, (total_rows, 1), 0)
    limit = jnp.zeros((total_rows, 1), jnp.int32)
    for u in range(NV):
        limit = jnp.where(idx // rows == u, counts[u], limit)
    alive = (lax.rem(idx, rows) // pdev < limit).astype(F32)
    a = act[...].reshape(total_rows, chans)
    tile = 512
    acc = jnp.zeros((total_rows, 128), F32)
    for t in range(dwidth // tile):
        sl = pl.ds(t * tile, tile)
        tok = jnp.dot(a, embed_w[:, sl], preferred_element_type=F32) + embed_b[:, sl]
        tok = (tok * alive).astype(BF16)
        tokens[:, sl] = tok
        tf = tok.astype(F32)
        for q in range(tile // 128):
            acc += tf[:, q * 128 : (q + 1) * 128]
    mu = jnp.sum(acc, axis=1, keepdims=True) * (1.0 / dwidth)
    acc = jnp.zeros((total_rows, 128), F32)
    for t in range(dwidth // tile):
        tf = tokens[:, pl.ds(t * tile, tile)].astype(F32) - mu
        for q in range(tile // 128):
            cut = tf[:, q * 128 : (q + 1) * 128]
            acc += cut * cut
    inv = lax.rsqrt(jnp.sum(acc, axis=1, keepdims=True) * (1.0 / dwidth) + 1e-06)
    for t in range(dwidth // tile):
        sl = pl.ds(t * tile, tile)
        tf = tokens[:, sl].astype(F32) - mu
        hidden[:, sl] = (tf * inv * (1.0 + scale[:, sl]) + shift[:, sl]).astype(BF16)
    cols = dwidth // NV
    resid[...] = tokens[:, pl.ds(pl.multiple_of(v * cols, 128), cols)]


def tokens_call(video, counts, conv_w, conv_b, norm_g, norm_b, embed_w, embed_b, shift, scale):
    rows, chans = video.shape
    dwidth = embed_w.shape[1]
    vm = pl.BlockSpec(memory_space=pltpu.VMEM)
    return pl.pallas_call(
        tokens_kernel,
        name="tokens",
        out_shape=(
            jax.ShapeDtypeStruct((NV * rows, dwidth), BF16),
            jax.ShapeDtypeStruct((NV * rows, dwidth // NV), BF16),
        ),
        in_specs=[vm, pl.BlockSpec(memory_space=pltpu.SMEM)] + [vm] * 8,
        out_specs=(vm, vm),
        scratch_shapes=[
            pltpu.VMEM((rows, chans), F32),
            pltpu.VMEM((3, chans, chans), BF16),
            pltpu.VMEM((3, chans, chans), BF16),
            pltpu.VMEM((NV, 2, chans), F32),
            pltpu.VMEM((NS, 2, chans), F32),
            pltpu.VMEM((NV, rows, chans), BF16),
            pltpu.VMEM((NV * rows, dwidth), BF16),
            pltpu.SemaphoreType.DMA((2,)),
            pltpu.SemaphoreType.DMA((NV,)),
            pltpu.SemaphoreType.DMA((NV,)),
            pltpu.SemaphoreType.DMA((NS,)),
            pltpu.SemaphoreType.DMA((NS,)),
            pltpu.SemaphoreType.DMA((9,)),
            pltpu.SemaphoreType.DMA((9,)),
        ],
        compiler_params=pltpu.CompilerParams(
            collective_id=0, has_side_effects=True, vmem_limit_bytes=40 * 2**20
        ),
    )(video, counts, conv_w, conv_b, norm_g, norm_b, embed_w, embed_b, shift, scale)

def flash_kernel(live, q_ref, k_ref, vt_ref, o_ref):
    nloc = q_ref.shape[1]
    q = q_ref[0]
    pdev = 16
    nseq = k_ref.shape[1]
    idx = lax.broadcasted_iota(jnp.int32, (nloc, 1), 0) // (4 * pdev)
    limit = jnp.zeros((nloc, 1), jnp.int32)
    for u in range(NV):
        limit = jnp.where(idx == u, live[u], limit)
    frame = lax.rem(lax.broadcasted_iota(jnp.int32, (nloc, 1), 0), 4 * pdev) // pdev
    bias = jnp.where(frame < limit, 0.0, -1e30)
    coef = math.log2(math.e) / math.sqrt(HD)

    def step(j, carry):
        m, l, acc = carry
        st = lax.dot_general(k_ref[0, j], q, (((1,), (1,)), ((), ())), preferred_element_type=F32)
        st = st * coef + bias
        new = jnp.maximum(m, jnp.max(st, axis=0, keepdims=True))
        alpha = jnp.exp2(m - new)
        p = jnp.exp2(st - new)
        l = l * alpha + jnp.sum(p, axis=0, keepdims=True)
        acc = acc * alpha + jnp.dot(vt_ref[0, j], p.astype(BF16), preferred_element_type=F32)
        return new, l, acc

    m0 = jnp.full((1, nloc), -1e30, F32)
    m, l, acc = lax.fori_loop(
        0, nseq, step, (m0, jnp.zeros((1, nloc), F32), jnp.zeros((HD, nloc), F32))
    )
    o_ref[...] = jnp.transpose(acc / l).astype(BF16)


def flash_call(live, q, k, vt):
    heads, nloc, _ = q.shape
    nseq = k.shape[1]
    return pl.pallas_call(
        flash_kernel,
        name="flash",
        grid=(heads,),
        out_shape=jax.ShapeDtypeStruct((nloc, heads * HD), BF16),
        in_specs=[
            pl.BlockSpec(memory_space=pltpu.SMEM),
            pl.BlockSpec((1, nloc, HD), lambda h: (h, 0, 0)),
            pl.BlockSpec((1, nseq, nloc, HD), lambda h: (h, 0, 0, 0)),
            pl.BlockSpec((1, nseq, HD, nloc), lambda h: (h, 0, 0, 0)),
        ],
        out_specs=pl.BlockSpec((nloc, HD), lambda h: (0, h)),
        compiler_params=pltpu.CompilerParams(vmem_limit_bytes=40 * 2**20),
    )(live, q, k, vt)


def head_norm(values, weights):
    return values * lax.rsqrt(jnp.mean(values * values, axis=-1, keepdims=True) + 1e-06) * weights


def body(
    video, frame_counts, conv_weight, conv_bias, norm_gain, norm_bias, embed_weight, embed_bias,
    shift, scale, gate, qkv_weight, q_gain, k_gain, out_weight,
):
    fdev, pdev, chans = video.shape
    me_vae = lax.axis_index("vae")
    row = lambda a: a.reshape(1, -1)
    hidden, resid = tokens_call(
        video.reshape(fdev * pdev, chans), frame_counts, conv_weight, row(conv_bias),
        row(norm_gain), row(norm_bias), embed_weight, row(embed_bias), row(shift), row(scale),
    )
    nloc, dwidth = hidden.shape
    cols = dwidth // NV
    w_cols = lax.all_to_all(
        out_weight.reshape(cols, NV, cols), "vae", split_axis=1, concat_axis=0, tiled=False
    ).reshape(dwidth, cols)
    w3 = jnp.transpose(qkv_weight, (1, 0, 2))
    heads = w3.shape[2] // HD
    proj = [jnp.dot(hidden, w3[i], preferred_element_type=F32) for i in range(3)]
    queries = head_norm(proj[0].reshape(nloc, heads, HD), q_gain).astype(BF16)
    keys = head_norm(proj[1].reshape(nloc, heads, HD), k_gain).astype(BF16)
    values = proj[2].reshape(nloc, heads, HD).astype(BF16)
    k_all = lax.all_gather(jnp.transpose(keys, (1, 0, 2)), "seq", axis=1)
    v_all = lax.all_gather(jnp.transpose(values, (1, 2, 0)), "seq", axis=1)
    o = flash_call(frame_counts, jnp.transpose(queries, (1, 0, 2)), k_all, v_all)
    o_all = lax.all_gather(o, "vae", axis=0)
    merged = jnp.transpose(o_all, (1, 0, 2)).reshape(nloc, dwidth)
    mixed = jnp.dot(merged, w_cols, preferred_element_type=F32)
    gate_part = lax.dynamic_slice_in_dim(gate, me_vae * cols, cols, 0)
    alive = (jnp.arange(fdev)[None, :] < frame_counts[:, None]).astype(F32)
    alive = jnp.broadcast_to(alive[:, :, None], (NV, fdev, pdev)).reshape(nloc, 1)
    result = ((resid.astype(F32) + gate_part * mixed) * alive).astype(BF16)
    return result.reshape(fdev * NV, pdev, cols)


def solution(mesh):
    in_specs = (
        P("vae", "seq", None), P(), P(), P(), P(), P(), P(), P(), P(), P(), P(),
        P(None, None, "vae"), P(), P(), P("vae", None),
    )
    return jax.shard_map(
        body, mesh=mesh, in_specs=in_specs, out_specs=P(None, "seq", "vae"), check_vma=False
    )
```

time: 401 us -> 303 us (0.76)
  Pallas kernels: 0 us -> 72.2 us
  blocking collectives: 65.9 us -> 0 us
  matrix products: 59.8 us -> 14.1 us
  other arithmetic: 43.8 us -> 1.22 us
  local copies, waits for them, and re-layouts: 71.5 us -> 55.2 us
    reduce_scatter x1 -> x0, waiting for transfers between devices: 90 us -> none  [body(): lax.psum_scatter(partial_out, 'vae', scatter_dimension=1, tiled=True)]
    pallas_call x0 -> x2, Pallas kernels: none -> 72.2 us  [the longest x1 38 us: tokens_call(): pl.pallas_call(tokens_kernel, name='tokens', out_shape=(jax.ShapeDtypeStr...]
    psum x1 -> x0, blocking collectives: 65.9 us -> none  [body(): first, second = lax.psum((first, second), ('vae', 'seq'))]
    all_gather x3, waiting for transfers between devices: 49.5 us -> 105 us  [the longest x1 47.3 us: body(): v_all = lax.all_gather(jnp.transpose(values, (1, 2, 0)), 'seq', axis=1)]
    gather x1 -> x0, local copies, waits for them, and re-layouts: 51.2 us -> none  [body(): alive = jnp.take(key_live, jnp.arange(length) % nloc) > 0.5]
    dot_general x8 -> x4, matrix products: 59.8 us -> 14.1 us  [the longest x3 9.8 us: body(): jnp.dot(hidden, w3[i], preferred_element_type=F32)]
    all_to_all x0 -> x1, waiting for transfers between devices: none -> 34.6 us  [body(): lax.all_to_all(out_weight.reshape(cols, NV, cols), 'vae', split_axis=1, c...]
    reduce_sum x8 -> x0, other arithmetic: 31 us -> none  [the longest x1 23.2 us: body(): summed = jnp.sum(weights, axis=-1)]
  transfers between devices with their start and end apart: 5 -> 4, of which waited for: 2 -> 4; matrix products, arithmetic and copies ran while one was open for 30% -> 11% of each run, Pallas kernels for 0% -> 0%
where the time goes in v1:
time: 303 us; the launch traced here: 302 us
  waiting for transfers between devices  140 us (46%)
  Pallas kernels  72.2 us (24%)
  local copies, waits for them, and re-layouts  55.2 us (18%)
  matrix products  14.1 us (5%)
  between operations  13.3 us (4%)
  starting transfers between devices  6.82 us (2%)
    all_gather x1, waiting for transfers between devices, body(): v_all = lax.all_gather(jnp.transpose(values, (1, 2, 0)), 'seq', axis=1)  47.3 us
    pallas_call x1, Pallas kernels, tokens_call(): pl.pallas_call(tokens_kernel, name='tokens', out_shape=(jax.ShapeDtypeStr...  38 us
    all_gather x1, waiting for transfers between devices, body(): o_all = lax.all_gather(o, 'vae', axis=0)  34.7 us
    all_to_all x1, waiting for transfers between devices, body(): lax.all_to_all(out_weight.reshape(cols, NV, cols), 'vae', split_axis=1, c...  34.6 us
    pallas_call x1, Pallas kernels, flash_call(): pl.pallas_call(flash_kernel, name='flash', grid=(heads,), out_shape=jax.S...  34.2 us
    all_gather x1, waiting for transfers between devices, body(): k_all = lax.all_gather(jnp.transpose(keys, (1, 0, 2)), 'seq', axis=1)  23 us
    dot_general x5, local copies, waits for them, and re-layouts, body(): jnp.dot(hidden, w3[i], preferred_element_type=F32)  20.8 us
    unnamed x41, local copies, waits for them, and re-layouts  10.3 us
  transfers between devices with their start and end apart: 4, of which 4 were waited for; matrix products, arithmetic and copies ran while one was open for 11% of the time, Pallas kernels for 0%

profile of v1, /device:TPU:0, one launch (start us, length us, event | category | flops | bytes accessed | tf_op | source)
XLA Modules:
  0.0 302.3 jit_solution(15827245913435063574)
XLA Ops:
  6.5 6.2 %slice_bitcast_fusion = (bf16[384,3072]{0,1:T(8,128)(2,1)}, bf16[384,3072]{0,1:T(8,128)(2,1)}, bf16[384,3072]{0,1:T(8,128)(2,1)}) fusion(bf16[3,3072,384]{2,1,0:T(8,128)(2,1)} %bitcast.86), kind=kLoop, calls=%fused_computation.6 | loop fusion | bytes 14155776 | tf_op jit(solution)/shard_map/dot_general | solution.py:325
  12.8 4.4 %copy.40 = bf16[384,3072]{1,0:T(8,128)(2,1)} copy(bf16[384,3072]{0,1:T(8,128)(2,1)} %get-tuple-element.10) | data formatting | bytes 4718592 | tf_op jit(solution)/shard_map/dot_general | solution.py:325
  17.4 1.9 copy-done.3
  19.2 38.0 %tokens.1 = (bf16[512,3072]{1,0:T(8,128)(2,1)S(1)}, bf16[512,384]{1,0:T(8,128)(2,1)S(1)}) custom-call(f32[64,512]{1,0:T(8,128)S(1)} %bitcast.78, s32[8]{0:T(128)S(1)} %copy-done.8, f32[3,512,512]{2,1,0:T(8,128)S(1)} %copy-done.2, f32[1,512]{1,0:T(1,128)S(1)} %bitcast.82, f32[1,512]{1,0:T(1,128)S(1)} %bitcast.83, f32[1,512]{1,0:T(1,128)S(1)} %bitcast.84, ...), custom_call_target="tpu_custom_call" | custom-call | tf_op jit(solution)/shard_map/tokens/pallas_call | solution.py:223
  57.3 1.4 multiply_reduce_fusion
  60.0 4.4 %copy.42 = bf16[384,3072]{1,0:T(8,128)(2,1)} copy(bf16[384,3072]{0,1:T(8,128)(2,1)} %get-tuple-element.9) | data formatting | bytes 4718592 | tf_op jit(solution)/shard_map/dot_general | solution.py:325
  64.4 4.3 %fusion.12 = bf16[3,128,512]{1,2,0:T(8,128)(2,1)} fusion(bf16[3,128,3072]{2,1,0:T(8,128)(2,1)} %bitcast.92, bf16[512,3072]{1,0:T(8,128)(2,1)S(1)} %copy-done.13), kind=kOutput, calls=%fused_computation.14 | convolution fusion | flops 1208156160 | bytes 5898240 | tf_op jit(solution)/shard_map/dot_general | solution.py:325
  68.9 4.3 %copy.38 = bf16[384,3072]{1,0:T(8,128)(2,1)} copy(bf16[384,3072]{0,1:T(8,128)(2,1)} %get-tuple-element.11) | data formatting | bytes 4718592 | tf_op jit(solution)/shard_map/dot_general | solution.py:325
  73.2 4.1 %multiply_reduce_fusion.1 = (f32[512,3]{0,1:T(4,128)S(1)}, f32[512,3,128]{0,2,1:T(8,128)}) fusion(bf16[3,128,3072]{2,1,0:T(8,128)(2,1)} %bitcast.91, bf16[512,3072]{1,0:T(8,128)(2,1)S(1)} %copy-done.13), kind=kOutput, calls=%fused_computation.22 | convolution fusion | flops 1208351232 | bytes 6297600 | tf_op jit(solution)/shard_map/dot_general | solution.py:325
  77.4 1.4 copy.39
  79.1 23.0 %all-gather.7.cloned.1.call-done = bf16[3,8192,128]{1,2,0:T(8,128)(2,1)} async-done(((bf16[3,512,128]{1,2,0:T(8,128)(2,1)}), bf16[3,8192,128]{1,2,0:T(8,128)(2,1)}) %all-gather.7.cloned.1.call-update) | async-done | bytes 6291472 | tf_op jit(solution)/shard_map/all_gather | solution.py:329
  102.0 8.7 %copy.41 = bf16[3,8192,128]{2,1,0:T(8,128)(2,1)} copy(bf16[3,8192,128]{1,2,0:T(8,128)(2,1)} %all-gather.7.cloned.1.call-done) | data formatting | bytes 12582912 | tf_op jit(solution)/shard_map/all_gather | solution.py:329
  110.7 47.3 %all-gather.9.cloned.1.call-done = bf16[3,2048,512]{1,2,0:T(8,128)(2,1)} async-done(((bf16[3,128,512]{1,2,0:T(8,128)(2,1)}), bf16[3,2048,512]{1,2,0:T(8,128)(2,1)}) %all-gather.9.cloned.1.call-update) | async-done | bytes 6291472 | tf_op jit(solution)/shard_map/all_gather | solution.py:330
  158.0 8.6 %copy.43 = bf16[3,2048,512]{2,1,0:T(8,128)(2,1)} copy(bf16[3,2048,512]{1,2,0:T(8,128)(2,1)} %all-gather.9.cloned.1.call-done) | data formatting | bytes 12582912 | tf_op jit(solution)/shard_map/all_gather | solution.py:330
  166.6 2.8 copy-done
  169.4 2.8 copy-done.1
  172.2 34.2 %flash.1 = bf16[512,384]{1,0:T(8,128)(2,1)} custom-call(s32[8]{0:T(128)S(1)} %copy-done.8, bf16[3,512,128]{2,1,0:T(8,128)(2,1)S(1)} %fusion.18.q_ref, bf16[3,16,512,128]{3,2,1,0:T(8,128)(2,1)S(1)} %bitcast.76, bf16[3,16,128,512]{3,2,1,0:T(8,128)(2,1)S(1)} %bitcast.77), custom_call_target="tpu_custom_call" | custom-call | tf_op jit(solution)/shard_map/flash/pallas_call | solution.py:287
  206.4 2.5 copy.45
  208.9 6.5 %all-to-all-start = ((bf16[1,384,8,384]{1,3,0,2:T(8,128)(2,1)}), bf16[1,384,8,384]{1,3,0,2:T(8,128)(2,1)S(1)}, u32[]{:S(2)}, u32[]{:S(2)}) async-start(bf16[1,384,8,384]{1,3,0,2:T(8,128)(2,1)} %bitcast.85), calls=%async_computation | async-start | bytes 4718592 | tf_op jit(solution)/shard_map/all_to_all | solution.py:320
  216.4 34.6 %all-to-all-done = bf16[1,384,8,384]{1,3,0,2:T(8,128)(2,1)S(1)} async-done(((bf16[1,384,8,384]{1,3,0,2:T(8,128)(2,1)}), bf16[1,384,8,384]{1,3,0,2:T(8,128)(2,1)S(1)}, u32[]{:S(2)}, u32[]{:S(2)}) %all-to-all-start) | async-done | bytes 2359328 | tf_op jit(solution)/shard_map/all_to_all | solution.py:320
  251.0 2.6 copy.47
  253.6 34.7 %all-gather.11.cloned.1.call-done = bf16[4096,384]{1,0:T(8,128)(2,1)} async-done(((bf16[512,384]{1,0:T(8,128)(2,1)}), bf16[4096,384]{1,0:T(8,128)(2,1)}) %all-gather.11.cloned.1.call-update) | async-done | bytes 3145744 | tf_op jit(solution)/shard_map/all_gather | solution.py:332
  288.3 3.2 %copy.44 = bf16[8,512,384]{1,2,0:T(8,128)(2,1)S(1)} copy(bf16[8,512,384]{2,1,0:T(8,128)(2,1)} %bitcast.87) | data formatting | bytes 6291456 | tf_op jit(solution)/shard_map/all_gather | solution.py:332
  291.6 4.3 %fusion.8 = bf16[512,384]{1,0:T(8,128)(2,1)} fusion(bf16[512,3072]{0,1:T(8,128)(2,1)S(1)} %bitcast.88, bf16[3072,384]{1,0:T(8,128)(2,1)} %bitcast.89, bf16[512,384]{1,0:T(8,128)(2,1)S(1)} %copy-done.15, f32[512]{0:T(512)S(1)} %mul.76, f32[384]{0:T(512)S(1)} %dynamic_slice.3), kind=kOutput, calls=%fused_computation.12 | convolution fusion | flops 1208942592 | bytes 6295040 | tf_op jit(solution)/shard_map/dot_general | solution.py:334
  (51 shorter events, 2.9 us)
Async XLA Ops:
  6.5 95.5 %all-gather.7.cloned.1.call-start = ((), (), s32[]{:S(2)}) async-start(), calls=%async_computation.1 | async-start | bytes 6684672 | tf_op jit(solution)/shard_map/all_gather | solution.py:329
  12.8 4.5 %copy-start.2 = (f32[3,512,512]{2,1,0:T(8,128)S(1)}, f32[3,512,512]{2,1,0:T(8,128)}, u32[]{:S(2)}) copy-start(f32[3,512,512]{2,1,0:T(8,128)} %conv_w.1) | copy-start | bytes 9437188
  12.8 4.5 %copy-start.4 = (f32[4,16,512]{2,1,0:T(8,128)S(1)}, f32[4,16,512]{2,1,0:T(8,128)}, u32[]{:S(2)}) copy-start(f32[4,16,512]{2,1,0:T(8,128)} %param.15) | copy-start | bytes 393220
  12.8 4.5 %copy-start.5 = (f32[3072]{0:T(1024)S(1)}, f32[3072]{0:T(1024)}, u32[]{:S(2)}) copy-start(f32[3072]{0:T(1024)} %param.22) | copy-start | bytes 36868
  12.8 4.5 %copy-start.6 = (f32[3072]{0:T(1024)S(1)}, f32[3072]{0:T(1024)}, u32[]{:S(2)}) copy-start(f32[3072]{0:T(1024)} %param.23) | copy-start | bytes 36868
  12.8 4.5 %copy-start.7 = (f32[3072]{0:T(1024)S(1)}, f32[3072]{0:T(1024)}, u32[]{:S(2)}) copy-start(f32[3072]{0:T(1024)} %param.24) | copy-start | bytes 36868
  12.8 4.5 %copy-start.8 = (s32[8]{0:T(128)S(1)}, s32[8]{0:T(128)}, u32[]{:S(2)}) copy-start(s32[8]{0:T(128)} %live.1) | copy-start | bytes 100
  12.8 4.5 %copy-start.9 = (f32[512]{0:T(512)S(1)}, f32[512]{0:T(512)}, u32[]{:S(2)}) copy-start(f32[512]{0:T(512)} %param.18) | copy-start | bytes 6148
  12.8 4.5 %copy-start.10 = (f32[512]{0:T(512)S(1)}, f32[512]{0:T(512)}, u32[]{:S(2)}) copy-start(f32[512]{0:T(512)} %param.19) | copy-start | bytes 6148
  12.8 4.5 %copy-start.11 = (f32[512]{0:T(512)S(1)}, f32[512]{0:T(512)}, u32[]{:S(2)}) copy-start(f32[512]{0:T(512)} %param.20) | copy-start | bytes 6148
  17.3 1.9 copy-start.3
  19.2 38.0 %copy-start.17 = (bf16[384,3072]{1,0:T(8,128)(2,1)S(1)}, bf16[384,3072]{1,0:T(8,128)(2,1)}, u32[]{:S(2)}) copy-start(bf16[384,3072]{1,0:T(8,128)(2,1)} %copy.40) | copy-start | bytes 7077892
  57.2 1.7 copy-start.12
  57.2 1.8 copy-start.14
  57.3 1.8 copy-start.18
  59.9 98.0 %all-gather.9.cloned.1.call-start = ((), (), s32[]{:S(2)}) async-start(), calls=%async_computation.2 | async-start | bytes 6684672 | tf_op jit(solution)/shard_map/all_gather | solution.py:330
  60.0 4.5 %copy-start.13 = (bf16[512,3072]{1,0:T(8,128)(2,1)S(1)}, bf16[512,3072]{1,0:T(8,128)(2,1)}, u32[]{:S(2)}) copy-start(bf16[512,3072]{1,0:T(8,128)(2,1)} %copy-done.12) | copy-start | bytes 9437188
  68.7 219.6 %all-gather.11.cloned.1.call-start = ((), (), s32[]{:S(2)}) async-start(), calls=%async_computation.3 | async-start | bytes 3538944 | tf_op jit(solution)/shard_map/all_gather | solution.py:332
  73.2 5.5 %copy-start.19 = (f32[128]{0:T(128)S(1)}, f32[128]{0:T(128)}, u32[]{:S(2)}) copy-start(f32[128]{0:T(128)} %param.27) | copy-start | bytes 1540
  166.6 2.8 copy-start
  169.4 2.8 copy-start.1
  172.2 34.2 %copy-start.16 = (bf16[384,3072]{1,0:T(8,128)(2,1)S(1)}, bf16[384,3072]{1,0:T(8,128)(2,1)}, u32[]{:S(2)}) copy-start(bf16[384,3072]{1,0:T(8,128)(2,1)} %param.29) | copy-start | bytes 7077892
  208.9 42.1 %all-to-all-start = ((bf16[1,384,8,384]{1,3,0,2:T(8,128)(2,1)}), bf16[1,384,8,384]{1,3,0,2:T(8,128)(2,1)S(1)}, u32[]{:S(2)}, u32[]{:S(2)}) async-start(bf16[1,384,8,384]{1,3,0,2:T(8,128)(2,1)} %bitcast.85), calls=%async_computation | async-start | bytes 4718592 | tf_op jit(solution)/shard_map/all_to_all | solution.py:320
  288.3 3.2 %copy-start.15 = (bf16[512,384]{1,0:T(8,128)(2,1)S(1)}, bf16[512,384]{1,0:T(8,128)(2,1)}, u32[]{:S(2)}) copy-start(bf16[512,384]{1,0:T(8,128)(2,1)} %copy-done.14) | copy-start | bytes 1179652
Sparse Core Ops, SparseCore 0:
  60.1 41.9 all-gather.6
  103.7 54.2 all-gather.8
  206.5 81.7 all-gather.10

commit v2 on v1

v2 whole, which is shorter than its diff:
```python
import functools
import math

import jax
import jax.numpy as jnp
from jax import lax
from jax.experimental import pallas as pl
from jax.experimental.pallas import tpu as pltpu
from jax.sharding import PartitionSpec as P

GROUPS = 32
HD = 128
NV = 8
NS = 16
F32 = jnp.float32
BF16 = jnp.bfloat16
MESH = pl.DeviceIdType.MESH


def mod(a, n):
    return lax.rem(a + n, n)


def fused_kernel(
    video, counts, conv_w_hbm, conv_b, norm_g, norm_b, embed_w_hbm, embed_b, shift, scale,
    gate, w3_hbm, q_gain, k_gain, out_w,
    result,
    conv_w, embed_w, w3,
    halo, w_hi, w_lo, sums_v, sums_s, act, tokens, hidden,
    kbuf, vbuf, qbuf, obuf, wcols,
    load_sem, halo_sem, ssem1, rsem1, ssem2, rsem2, asend, arecv,
    wsend, wrecv, ksend, krecv, vrecv, osend, orecv,
):
    v = lax.axis_index("vae")
    s = lax.axis_index("seq")
    rows, chans = video.shape
    pdev = 16
    width = chans // GROUPS
    dwidth = embed_b.shape[1]
    cols = dwidth // NV
    heads = cols // HD
    nloc = NV * rows

    loads = [
        pltpu.make_async_copy(conv_w_hbm, conv_w, load_sem.at[0]),
        pltpu.make_async_copy(embed_w_hbm, embed_w, load_sem.at[1]),
        pltpu.make_async_copy(w3_hbm, w3, load_sem.at[2]),
    ]
    for c in loads:
        c.start()

    xl = s // 8
    y = lax.rem(s, 8) // 2
    core = lax.rem(s, 2)
    r = lax.rem(s, 8)

    def place(dx, dy, dc):
        return mod(xl + dx, 2) * 8 + mod(y + dy, 4) * 2 + mod(core + dc, 2)

    part_rows = cols // 8
    own_w = pltpu.make_async_copy(
        out_w.at[pl.ds(r * part_rows, part_rows), pl.ds(pl.multiple_of(v * cols, 128), cols)],
        wcols.at[v, pl.ds(r * part_rows, part_rows)],
        load_sem.at[3],
    )
    own_w.start()

    barrier = pltpu.get_barrier_semaphore()
    for d in range(1, NV):
        pl.semaphore_signal(barrier, inc=1, device_id=(mod(v + d, NV), s), device_id_type=MESH)
    for d in range(1, NS):
        pl.semaphore_signal(barrier, inc=1, device_id=(v, mod(s + d, NS)), device_id_type=MESH)

    @pl.when(v == 0)
    def _():
        halo[...] = jnp.zeros_like(halo)

    pl.semaphore_wait(barrier, NV - 1 + NS - 1)
    halo_copy = pltpu.make_async_remote_copy(
        src_ref=video, dst_ref=halo, send_sem=halo_sem.at[0], recv_sem=halo_sem.at[1],
        device_id=(mod(v + 1, NV), s), device_id_type=MESH,
    )

    @pl.when(v < NV - 1)
    def _():
        halo_copy.start()

    w_first = []
    for d in range(1, NV):
        u = mod(v + d, NV)
        c = pltpu.make_async_remote_copy(
            src_ref=out_w.at[
                pl.ds(r * part_rows, part_rows), pl.ds(pl.multiple_of(u * cols, 128), cols)
            ],
            dst_ref=wcols.at[v, pl.ds(r * part_rows, part_rows)],
            send_sem=wsend.at[d], recv_sem=wrecv.at[d],
            device_id=(u, s), device_id_type=MESH,
        )
        c.start()
        w_first.append(c)

    loads[0].wait()
    for tap in range(3):
        w = conv_w[tap]
        hi = w.astype(BF16)
        w_hi[tap] = hi
        w_lo[tap] = (w - hi.astype(F32)).astype(BF16)

    mine = counts[v]
    before = counts[jnp.maximum(v - 1, 0)]

    @pl.when(v > 0)
    def _():
        halo_copy.wait_recv()

    prior = jnp.where(
        before == 2, halo[0:32], jnp.where(before == 3, halo[16:48], halo[32:64])
    )
    ext = jnp.concatenate([prior, video[...]], 0)
    e_hi = ext.astype(BF16)
    e_lo = (ext - e_hi.astype(F32)).astype(BF16)
    both = jnp.zeros((2 * rows, chans), F32)
    low = jnp.zeros((rows, chans), F32)
    for tap in range(3):
        a = 32 - 16 * tap
        x_hi = e_hi[a : a + rows]
        both += jnp.dot(
            jnp.concatenate([x_hi, e_lo[a : a + rows]], 0), w_hi[tap], preferred_element_type=F32
        )
        low += jnp.dot(x_hi, w_lo[tap], preferred_element_type=F32)
    conv = both[:rows] + (both[rows:] + low) + conv_b[...]
    row_frame = lax.broadcasted_iota(jnp.int32, (rows, chans), 0) // pdev
    masked = jnp.where(row_frame < mine, conv, 0.0)
    first = jnp.sum(masked, axis=0, keepdims=True)
    second = jnp.sum(masked * conv, axis=0, keepdims=True)
    sums_v[v] = jnp.concatenate([first, second], 0)

    @pl.when(v < NV - 1)
    def _():
        halo_copy.wait_send()

    sends = []
    for d in range(1, NV):
        c = pltpu.make_async_remote_copy(
            src_ref=sums_v.at[v], dst_ref=sums_v.at[v], send_sem=ssem1.at[d], recv_sem=rsem1.at[d],
            device_id=(mod(v + d, NV), s), device_id_type=MESH,
        )
        c.start()
        sends.append(c)
    gi = lax.broadcasted_iota(jnp.int32, (chans, chans), 0) // width
    gj = lax.broadcasted_iota(jnp.int32, (chans, chans), 1) // width
    same = jnp.where(gi == gj, 1.0, 0.0).astype(BF16)
    live = counts[0]
    for u in range(1, NV):
        live += counts[u]
    own_w.wait()
    for c in w_first:
        c.wait()
    for c in sends:
        c.wait()
    total = sums_v[0]
    for u in range(1, NV):
        total += sums_v[u]
    sums_s[s] = total
    sends = []
    for d in range(1, NS):
        c = pltpu.make_async_remote_copy(
            src_ref=sums_s.at[s], dst_ref=sums_s.at[s], send_sem=ssem2.at[d], recv_sem=rsem2.at[d],
            device_id=(v, mod(s + d, NS)), device_id_type=MESH,
        )
        c.start()
        sends.append(c)

    def w_hop(dy, lo, n, dev, sem):
        rr = mod(y + dy, 4) * 2 + core
        ref = wcols.at[pl.ds(lo, n), pl.ds(rr * part_rows, part_rows)]
        return pltpu.make_async_remote_copy(
            src_ref=ref, dst_ref=ref, send_sem=wsend.at[sem], recv_sem=wrecv.at[sem],
            device_id=(v, dev), device_id_type=MESH,
        )

    partner = place(0, 0, 1)
    y_up, y_dn = place(0, 1, 0), place(0, 3, 0)
    w_up = w_hop(0, 0, NV, y_up, 8)
    w_dn = w_hop(0, 0, NV, y_dn, 9)
    w_pt = w_hop(0, 0, NV, partner, 10)

    for c in sends:
        c.wait()
    w_up.start()
    w_dn.start()
    w_pt.start()
    total = sums_s[0]
    for u in range(1, NS):
        total += sums_s[u]
    p1 = total.astype(BF16)
    r1 = total - p1.astype(F32)
    p2 = r1.astype(BF16)
    p3 = (r1 - p2.astype(F32)).astype(BF16)
    grouped = (
        jnp.dot(p3, same, preferred_element_type=F32)
        + jnp.dot(p2, same, preferred_element_type=F32)
        + jnp.dot(p1, same, preferred_element_type=F32)
    )
    number = live.astype(F32) * (pdev * NS * width)
    mean = grouped[0:1] / number
    var = grouped[1:2] / number - mean * mean
    yv = (conv - mean) * lax.rsqrt(var + 1e-06) * norm_g[...] + norm_b[...]
    act[v] = (yv / (1.0 + jnp.exp(-yv))).astype(BF16)

    far = mod(v + 4, NV)
    base = (v // 4) * 4
    fbase = 4 - base
    z = lax.rem(v, 4)
    up, down = mod(z + 1, 4), mod(z - 1, 4)

    def vae_gather(view, n, send, recv):
        half = n // 2

        def hop(slot, lo, cnt, dev, sem):
            ref = view(slot, lo, cnt)
            return pltpu.make_async_remote_copy(
                src_ref=ref, dst_ref=ref, send_sem=send(sem), recv_sem=recv(sem),
                device_id=(dev, s), device_id_type=MESH,
            )

        far_c = hop(v, 0, n, far, 0)
        up_c = hop(v, 0, n, base + up, 1)
        dn_c = hop(v, 0, n, base + down, 2)
        fup_c = hop(far, 0, n, base + up, 3)
        fdn_c = hop(far, 0, n, base + down, 4)
        o1 = hop(base + down, 0, half, base + up, 5)
        o2 = hop(base + up, half, half, base + down, 6)
        o3 = hop(fbase + down, 0, half, base + up, 7)
        o4 = hop(fbase + up, half, half, base + down, 8)

        def one():
            far_c.start()
            up_c.start()
            dn_c.start()

        def two():
            far_c.wait_recv()
            fup_c.start()
            fdn_c.start()
            up_c.wait_recv()
            o1.start()
            dn_c.wait_recv()
            o2.start()

        def three():
            fup_c.wait_recv()
            o3.start()
            fdn_c.wait_recv()
            o4.start()

        def four():
            for c in (o1, o2, o3, o4):
                c.wait_recv()

        def five():
            for c in (far_c, up_c, dn_c, fup_c, fdn_c, o1, o2, o3, o4):
                c.wait_send()

        return one, two, three, four, five

    g = vae_gather(
        lambda slot, lo, n: act.at[slot, pl.ds(lo, n)],
        rows,
        lambda i: asend.at[i],
        lambda i: arecv.at[i],
    )
    g[0]()
    g[1]()
    w_up.wait_recv()
    w_r1 = w_hop(3, 0, NV // 2, y_up, 11)
    w_p1 = w_hop(3, 0, NV, partner, 12)
    w_r1.start()
    w_p1.start()
    w_dn.wait_recv()
    w_r2 = w_hop(1, NV // 2, NV // 2, y_dn, 13)
    w_p2 = w_hop(1, 0, NV, partner, 14)
    w_r2.start()
    w_p2.start()
    g[2]()
    g[3]()
    g[4]()

    idx = lax.broadcasted_iota(jnp.int32, (nloc, 1), 0)
    limit = jnp.zeros((nloc, 1), jnp.int32)
    for u in range(NV):
        limit = jnp.where(idx // rows == u, counts[u], limit)
    alive = (lax.rem(idx, rows) // pdev < limit).astype(F32)
    loads[1].wait()
    a = act[...].reshape(nloc, chans)
    tile = 512
    acc = jnp.zeros((nloc, 128), F32)
    for t in range(dwidth // tile):
        sl = pl.ds(t * tile, tile)
        tok = jnp.dot(a, embed_w[:, sl], preferred_element_type=F32) + embed_b[:, sl]
        tok = (tok * alive).astype(BF16)
        tokens[:, sl] = tok
        tf = tok.astype(F32)
        for q in range(tile // 128):
            acc += tf[:, q * 128 : (q + 1) * 128]
    mu = jnp.sum(acc, axis=1, keepdims=True) * (1.0 / dwidth)
    acc = jnp.zeros((nloc, 128), F32)
    for t in range(dwidth // tile):
        tf = tokens[:, pl.ds(t * tile, tile)].astype(F32) - mu
        for q in range(tile // 128):
            cut = tf[:, q * 128 : (q + 1) * 128]
            acc += cut * cut
    inv = lax.rsqrt(jnp.sum(acc, axis=1, keepdims=True) * (1.0 / dwidth) + 1e-06)
    for t in range(dwidth // tile):
        sl = pl.ds(t * tile, tile)
        tf = tokens[:, sl].astype(F32) - mu
        hidden[:, sl] = (tf * inv * (1.0 + scale[:, sl]) + shift[:, sl]).astype(BF16)

    x_to = place(1, 0, 0)

    def kv_hop(h, is_v, slot, part, dev, sem):
        buf, rec = (vbuf, vrecv) if is_v else (kbuf, krecv)
        n = HD if is_v else nloc
        if part is None:
            ref, ri = buf.at[h, slot], 0
        else:
            ref, ri = buf.at[h, slot, pl.ds(part * (n // 2), n // 2)], part
        return pltpu.make_async_remote_copy(
            src_ref=ref, dst_ref=ref, send_sem=ksend.at[h, sem], recv_sem=rec.at[h, slot, ri],
            device_id=(v, dev), device_id_type=MESH,
        )

    SENDS = {
        1: [
            (iv, (0, 0, 0), None, dev)
            for iv in (0, 1)
            for dev in ("x", "up", "dn", "pt")
        ],
        2: [
            (0, (1, 0, 0), None, "up"),
            (0, (1, 0, 0), None, "dn"),
            (0, (1, 0, 0), None, "pt"),
            (0, (0, 3, 0), 0, "up"),
            (0, (0, 3, 0), None, "pt"),
            (0, (0, 1, 0), 1, "dn"),
            (0, (0, 1, 0), None, "pt"),
            (1, (0, 3, 0), 0, "up"),
            (1, (0, 3, 0), None, "x"),
            (1, (0, 3, 0), None, "pt"),
            (1, (0, 1, 0), 1, "dn"),
            (1, (0, 1, 0), None, "x"),
            (1, (0, 1, 0), None, "pt"),
            (1, (1, 0, 0), None, "pt"),
        ],
        3: [
            (0, (1, 3, 0), 0, "up"),
            (0, (1, 3, 0), None, "pt"),
            (0, (1, 1, 0), 1, "dn"),
            (0, (1, 1, 0), None, "pt"),
            (0, (0, 2, 0), None, "pt"),
            (1, (0, 2, 0), None, "x"),
            (1, (0, 2, 0), None, "pt"),
            (1, (1, 3, 0), None, "pt"),
            (1, (1, 1, 0), None, "pt"),
        ],
        4: [
            (0, (1, 2, 0), None, "pt"),
            (1, (1, 2, 0), None, "pt"),
        ],
    }
    devs = {"x": x_to, "up": y_up, "dn": y_dn, "pt": partner}

    def arrived(h, iv, where):
        halves = where[1] == 2 and where[2] == 0 and not (iv and where[0] == 1)
        slot = place(*where)
        for part in ((0, 1) if halves else (None,)):
            kv_hop(h, iv, slot, part, partner, 0).wait_recv()

    first_sem = {1: 0, 2: 8, 3: 22, 4: 31}

    def stage(n, h):
        seen = set()
        for i, (iv, where, part, dev) in enumerate(SENDS[n]):
            if n > 1 and (iv, where) not in seen:
                seen.add((iv, where))
                arrived(h, iv, where)
            kv_hop(h, iv, place(*where), part, devs[dev], first_sem[n] + i).start()

    loads[2].wait()
    hid = hidden[...]
    kp = jnp.dot(hid, w3[1], preferred_element_type=F32)
    for h in range(heads):
        x = kp[:, h * HD : (h + 1) * HD]
        x = x * lax.rsqrt(jnp.mean(x * x, axis=-1, keepdims=True) + 1e-06) * k_gain[...]
        kbuf[h, s] = x.astype(BF16)
    vp = jnp.dot(hid, w3[2], preferred_element_type=F32)
    for h in range(heads):
        vbuf[h, s] = jnp.transpose(vp[:, h * HD : (h + 1) * HD]).astype(BF16)
        if h < 2:
            stage(1, h)
    qp = jnp.dot(hid, w3[0], preferred_element_type=F32)
    for h in range(heads):
        x = qp[:, h * HD : (h + 1) * HD]
        x = x * lax.rsqrt(jnp.mean(x * x, axis=-1, keepdims=True) + 1e-06) * q_gain[...]
        qbuf[h] = jnp.transpose(x).astype(BF16)
    stage(2, 0)
    stage(1, 2)
    stage(3, 0)

    w_r1.wait_recv()
    w_r2.wait_recv()
    w_p3 = w_hop(2, 0, NV, partner, 15)
    w_p3.start()

    bias = jnp.where(alive > 0.5, 0.0, -1e30)
    coef = math.log2(math.e) / math.sqrt(HD)

    def attend(h, g, carry):
        for dy in range(4):
            for iv in (0, 1):
                arrived(h, iv, (g, dy, 1))
        q = qbuf[h]

        def step(j, carry):
            m, l, acc = carry
            slot = mod(xl + g, 2) * 8 + lax.rem(y + j // 2, 4) * 2 + lax.rem(core + j, 2)
            st = jnp.dot(kbuf[h, slot], q, preferred_element_type=F32)
            st = st * coef + bias
            new = jnp.maximum(m, jnp.max(st, axis=0, keepdims=True))
            alpha = jnp.exp2(m - new)
            p = jnp.exp2(st - new)
            l = l * alpha + jnp.sum(p, axis=0, keepdims=True)
            acc = acc * alpha + jnp.dot(
                vbuf[h, slot], p.astype(BF16), preferred_element_type=F32
            )
            return new, l, acc

        return lax.fori_loop(0, 8, step, carry)

    def fresh():
        return (
            jnp.full((1, nloc), -1e30, F32),
            jnp.zeros((1, nloc), F32),
            jnp.zeros((HD, nloc), F32),
        )

    og = []
    for h in range(heads):
        og.append(
            vae_gather(
                lambda slot, lo, n, h=h: obuf.at[slot, pl.ds(lo, n), pl.ds(h * HD, HD)],
                nloc,
                lambda i, h=h: osend.at[h, i],
                lambda i, h=h: orecv.at[h, i],
            )
        )

    def finish(h, carry):
        m, l, acc = carry
        obuf[v, :, pl.ds(h * HD, HD)] = jnp.transpose(acc / l).astype(BF16)

    c = attend(0, 0, fresh())
    stage(2, 1)
    stage(4, 0)
    c = attend(0, 1, c)
    stage(3, 1)
    stage(2, 2)
    finish(0, c)
    og[0][0]()
    c = attend(1, 0, fresh())
    stage(4, 1)
    stage(3, 2)
    og[0][1]()
    c = attend(1, 1, c)
    og[0][2]()
    finish(1, c)
    og[1][0]()
    c = attend(2, 0, fresh())
    stage(4, 2)
    og[1][1]()
    c = attend(2, 1, c)
    og[1][2]()
    finish(2, c)
    og[2][0]()
    w_pt.wait_recv()
    w_p1.wait_recv()
    w_p2.wait_recv()
    w_p3.wait_recv()
    og[0][3]()
    og[1][3]()
    og[2][1]()

    def project(lo, n, start):
        def add(u, acc):
            return acc + jnp.dot(
                obuf[u, :, pl.ds(lo, n)], wcols[u, pl.ds(lo, n), :], preferred_element_type=F32
            )

        return lax.fori_loop(0, NV, add, start)

    mixed = project(0, 2 * HD, jnp.zeros((nloc, cols), F32))
    og[2][2]()
    og[2][3]()
    mixed = project(2 * HD, HD, mixed)
    here = pl.ds(pl.multiple_of(v * cols, 128), cols)
    resid = tokens[:, here].astype(F32)
    result[...] = ((resid + gate[:, here] * mixed) * alive).astype(BF16)

    for h in range(heads):
        og[h][4]()
        for n in (1, 2, 3, 4):
            for i, (iv, where, part, dev) in enumerate(SENDS[n]):
                kv_hop(h, iv, place(*where), part, devs[dev], first_sem[n] + i).wait_send()
    for c in (w_up, w_dn, w_pt, w_r1, w_p1, w_r2, w_p2, w_p3):
        c.wait_send()


def body(
    video, frame_counts, conv_weight, conv_bias, norm_gain, norm_bias, embed_weight, embed_bias,
    shift, scale, gate, qkv_weight, q_gain, k_gain, out_weight,
):
    fdev, pdev, chans = video.shape
    rows = fdev * pdev
    dwidth = embed_weight.shape[1]
    cols = qkv_weight.shape[2]
    heads = cols // HD
    nloc = NV * rows
    vm = pl.BlockSpec(memory_space=pltpu.VMEM)
    hbm = pl.BlockSpec(memory_space=pl.ANY)
    dma = pltpu.SemaphoreType.DMA
    out = pl.pallas_call(
        fused_kernel,
        name="fused",
        out_shape=jax.ShapeDtypeStruct((nloc, cols), BF16),
        in_specs=[
            vm, pl.BlockSpec(memory_space=pltpu.SMEM), hbm, vm, vm, vm, hbm, vm, vm, vm, vm, hbm,
            vm, vm, hbm,
        ],
        out_specs=vm,
        scratch_shapes=[
            pltpu.VMEM((3, chans, chans), F32),
            pltpu.VMEM((chans, dwidth), BF16),
            pltpu.VMEM((3, dwidth, cols), BF16),
            pltpu.VMEM((rows, chans), F32),
            pltpu.VMEM((3, chans, chans), BF16),
            pltpu.VMEM((3, chans, chans), BF16),
            pltpu.VMEM((NV, 2, chans), F32),
            pltpu.VMEM((NS, 2, chans), F32),
            pltpu.VMEM((NV, rows, chans), BF16),
            pltpu.VMEM((nloc, dwidth), BF16),
            pltpu.VMEM((nloc, dwidth), BF16),
            pltpu.VMEM((heads, NS, nloc, HD), BF16),
            pltpu.VMEM((heads, NS, HD, nloc), BF16),
            pltpu.VMEM((heads, HD, nloc), BF16),
            pltpu.VMEM((NV, nloc, cols), BF16),
            pltpu.VMEM((NV, cols, cols), BF16),
            dma((4,)),
            dma((2,)),
            dma((NV,)),
            dma((NV,)),
            dma((NS,)),
            dma((NS,)),
            dma((9,)),
            dma((9,)),
            dma((16,)),
            dma((16,)),
            dma((heads, 33)),
            dma((heads, NS, 2)),
            dma((heads, NS, 2)),
            dma((heads, 9)),
            dma((heads, 9)),
        ],
        compiler_params=pltpu.CompilerParams(
            collective_id=0, has_side_effects=True, vmem_limit_bytes=62 * 2**20
        ),
    )(
        video.reshape(rows, chans), frame_counts, conv_weight, conv_bias.reshape(1, -1),
        norm_gain.reshape(1, -1), norm_bias.reshape(1, -1), embed_weight,
        embed_bias.reshape(1, -1), shift.reshape(1, -1), scale.reshape(1, -1),
        gate.reshape(1, -1), jnp.transpose(qkv_weight, (1, 0, 2)), q_gain.reshape(1, -1),
        k_gain.reshape(1, -1), out_weight,
    )
    return out.reshape(fdev * NV, pdev, cols)


def solution(mesh):
    in_specs = (
        P("vae", "seq", None), P(), P(), P(), P(), P(), P(), P(), P(), P(), P(),
        P(None, None, "vae"), P(), P(), P("vae", None),
    )
    return jax.shard_map(
        body, mesh=mesh, in_specs=in_specs, out_specs=P(None, "seq", "vae"), check_vma=False
    )
```

time: 303 us -> 135 us (0.45)
  waiting for transfers between devices: 140 us -> 0 us
  Pallas kernels: 72.2 us -> 133 us
  local copies, waits for them, and re-layouts: 55.2 us -> 1.78 us
  matrix products: 14.1 us -> 0 us
  between operations: 13.3 us -> 0.01 us
  starting transfers between devices: 6.82 us -> 0 us
    all_gather x3 -> x0, waiting for transfers between devices: 105 us -> none  [the longest x1 47.3 us: body(): v_all = lax.all_gather(jnp.transpose(values, (1, 2, 0)), 'seq', axis=1)]
    pallas_call x2 -> x1, Pallas kernels: 72.2 us -> 133 us  [body(): pl.pallas_call(fused_kernel, name='fused', out_shape=jax.ShapeDtypeStruct...]
    all_to_all x1 -> x0, waiting for transfers between devices: 34.6 us -> none  [body(): lax.all_to_all(out_weight.reshape(cols, NV, cols), 'vae', split_axis=1, c...]
    dot_general x5 -> x0, local copies, waits for them, and re-layouts: 20.8 us -> none  [body(): jnp.dot(hidden, w3[i], preferred_element_type=F32)]
    all_gather x3 -> x0, local copies, waits for them, and re-layouts: 20.5 us -> none  [the longest x1 8.68 us: body(): k_all = lax.all_gather(jnp.transpose(keys, (1, 0, 2)), 'seq', axis=1)]
    dot_general x4 -> x0, matrix products: 14.1 us -> none  [the longest x3 9.8 us: body(): jnp.dot(hidden, w3[i], preferred_element_type=F32)]
    unnamed x41 -> x1, local copies, waits for them, and re-layouts: 10.3 us -> 1.78 us
    all_to_all x1 -> x0, starting transfers between devices: 6.55 us -> none  [body(): lax.all_to_all(out_weight.reshape(cols, NV, cols), 'vae', split_axis=1, c...]
  transfers between devices with their start and end apart: 4 -> 0, of which waited for: 4 -> 0; matrix products, arithmetic and copies ran while one was open for 11% -> 0% of each run, Pallas kernels for 0% -> 0%
where the time goes in v2:
time: 135 us; the launch traced here: 134 us
  Pallas kernels  133 us (99%)
  local copies, waits for them, and re-layouts  1.78 us (1%)
    pallas_call x1, Pallas kernels, body(): pl.pallas_call(fused_kernel, name='fused', out_shape=jax.ShapeDtypeStruct...  133 us

profile of v2, /device:TPU:0, one launch (start us, length us, event | category | flops | bytes accessed | tf_op | source)
XLA Modules:
  0.0 134.5 jit_solution(11652416994431945918)
XLA Ops:
  0.0 132.7 %fused.1 = bf16[512,384]{1,0:T(8,128)(2,1)} custom-call(f32[64,512]{1,0:T(8,128)} %bitcast.14, s32[8]{0:T(128)} %counts.1, f32[3,512,512]{2,1,0:T(8,128)} %conv_w_hbm.1, f32[1,512]{1,0:T(1,128)} %bitcast.19, f32[1,512]{1,0:T(1,128)} %bitcast.20, f32[1,512]{1,0:T(1,128)} %bitcast.21, bf16[512,3072]{1,0:T(8,128)(2,1)} %embed_w_hbm.1, f32[1,3072]{1,0:T(1,128)} %bitcast.15, ...), custom_call_target="tpu_custom_call" | custom-call | tf_op jit(solution)/shard_map/fused/pallas_call | solution.py:531
  132.7 1.8 %copy.17 = bf16[32,16,384]{2,1,0:T(8,128)(2,1)} copy(bf16[32,16,384]{2,1,0:T(8,128)(2,1)} %bitcast.13) | data formatting | bytes 786432

commit v3 on v2

--- a/solution.py
+++ b/solution.py
@@ -15,6 +15,7 @@
 F32 = jnp.float32
 BF16 = jnp.bfloat16
 MESH = pl.DeviceIdType.MESH
+UNROLL = 4
 
 
 def mod(a, n):
@@ -27,7 +28,7 @@
     result,
     conv_w, embed_w, w3,
     halo, w_hi, w_lo, sums_v, sums_s, act, tokens, hidden,
-    kbuf, vbuf, qbuf, obuf, wcols,
+    kbuf, vbuf, qbuf, obuf, wcols, score_a, score_b, k_tail,
     load_sem, halo_sem, ssem1, rsem1, ssem2, rsem2, asend, arecv,
     wsend, wrecv, ksend, krecv, vrecv, osend, orecv,
 ):
@@ -153,9 +154,6 @@
     live = counts[0]
     for u in range(1, NV):
         live += counts[u]
-    own_w.wait()
-    for c in w_first:
-        c.wait()
     for c in sends:
         c.wait()
     total = sums_v[0]
@@ -185,6 +183,9 @@
     w_dn = w_hop(0, 0, NV, y_dn, 9)
     w_pt = w_hop(0, 0, NV, partner, 10)
 
+    own_w.wait()
+    for c in w_first:
+        c.wait()
     for c in sends:
         c.wait()
     w_up.start()
@@ -272,16 +273,6 @@
     )
     g[0]()
     g[1]()
-    w_up.wait_recv()
-    w_r1 = w_hop(3, 0, NV // 2, y_up, 11)
-    w_p1 = w_hop(3, 0, NV, partner, 12)
-    w_r1.start()
-    w_p1.start()
-    w_dn.wait_recv()
-    w_r2 = w_hop(1, NV // 2, NV // 2, y_dn, 13)
-    w_p2 = w_hop(1, 0, NV, partner, 14)
-    w_r2.start()
-    w_p2.start()
     g[2]()
     g[3]()
     g[4]()
@@ -303,6 +294,16 @@
         tf = tok.astype(F32)
         for q in range(tile // 128):
             acc += tf[:, q * 128 : (q + 1) * 128]
+    w_up.wait_recv()
+    w_r1 = w_hop(3, 0, NV // 2, y_up, 11)
+    w_p1 = w_hop(3, 0, NV, partner, 12)
+    w_r1.start()
+    w_p1.start()
+    w_dn.wait_recv()
+    w_r2 = w_hop(1, NV // 2, NV // 2, y_dn, 13)
+    w_p2 = w_hop(1, 0, NV, partner, 14)
+    w_r2.start()
+    w_p2.start()
     mu = jnp.sum(acc, axis=1, keepdims=True) * (1.0 / dwidth)
     acc = jnp.zeros((nloc, 128), F32)
     for t in range(dwidth // tile):
@@ -330,61 +331,56 @@
             device_id=(v, dev), device_id_type=MESH,
         )
 
-    SENDS = {
-        1: [
-            (iv, (0, 0, 0), None, dev)
+    own = (0, 0, 0)
+    X_FIRST = {
+        1: [(own, None, dev) for dev in ("x", "up", "dn", "pt")],
+        2: [((1, 0, 0), None, dev) for dev in ("up", "dn", "pt")]
+        + [((0, 3, 0), 0, "up"), ((0, 3, 0), None, "pt")]
+        + [((0, 1, 0), 1, "dn"), ((0, 1, 0), None, "pt")],
+        3: [((1, 3, 0), 0, "up"), ((1, 3, 0), None, "pt")]
+        + [((1, 1, 0), 1, "dn"), ((1, 1, 0), None, "pt"), ((0, 2, 0), None, "pt")],
+        4: [((1, 2, 0), None, "pt")],
+    }
+    Y_FIRST = {
+        1: X_FIRST[1],
+        2: [((0, 3, 0), 0, "up"), ((0, 3, 0), None, "x"), ((0, 3, 0), None, "pt")]
+        + [((0, 1, 0), 1, "dn"), ((0, 1, 0), None, "x"), ((0, 1, 0), None, "pt")]
+        + [((1, 0, 0), None, "pt")],
+        3: [((0, 2, 0), None, "x"), ((0, 2, 0), None, "pt")]
+        + [((1, 3, 0), None, "pt"), ((1, 1, 0), None, "pt")],
+        4: [((1, 2, 0), None, "pt")],
+    }
+
+    def x_first(h, iv):
+        return iv == 0 or h >= 1
+
+    def sends_of(h, n):
+        return [
+            (iv, *entry)
             for iv in (0, 1)
-            for dev in ("x", "up", "dn", "pt")
-        ],
-        2: [
-            (0, (1, 0, 0), None, "up"),
-            (0, (1, 0, 0), None, "dn"),
-            (0, (1, 0, 0), None, "pt"),
-            (0, (0, 3, 0), 0, "up"),
-            (0, (0, 3, 0), None, "pt"),
-            (0, (0, 1, 0), 1, "dn"),
-            (0, (0, 1, 0), None, "pt"),
-            (1, (0, 3, 0), 0, "up"),
-            (1, (0, 3, 0), None, "x"),
-            (1, (0, 3, 0), None, "pt"),
-            (1, (0, 1, 0), 1, "dn"),
-            (1, (0, 1, 0), None, "x"),
-            (1, (0, 1, 0), None, "pt"),
-            (1, (1, 0, 0), None, "pt"),
-        ],
-        3: [
-            (0, (1, 3, 0), 0, "up"),
-            (0, (1, 3, 0), None, "pt"),
-            (0, (1, 1, 0), 1, "dn"),
-            (0, (1, 1, 0), None, "pt"),
-            (0, (0, 2, 0), None, "pt"),
-            (1, (0, 2, 0), None, "x"),
-            (1, (0, 2, 0), None, "pt"),
-            (1, (1, 3, 0), None, "pt"),
-            (1, (1, 1, 0), None, "pt"),
-        ],
-        4: [
-            (0, (1, 2, 0), None, "pt"),
-            (1, (1, 2, 0), None, "pt"),
-        ],
-    }
+            for entry in (X_FIRST if x_first(h, iv) else Y_FIRST)[n]
+        ]
+
     devs = {"x": x_to, "up": y_up, "dn": y_dn, "pt": partner}
 
     def arrived(h, iv, where):
-        halves = where[1] == 2 and where[2] == 0 and not (iv and where[0] == 1)
+        halves = where[1] == 2 and where[2] == 0 and (x_first(h, iv) or where[0] == 0)
         slot = place(*where)
         for part in ((0, 1) if halves else (None,)):
             kv_hop(h, iv, slot, part, partner, 0).wait_recv()
 
-    first_sem = {1: 0, 2: 8, 3: 22, 4: 31}
-
-    def stage(n, h):
+    def first_sem(h, n):
+        return sum(len(sends_of(h, k)) for k in range(1, n))
+
+    def stage(n, h, only=None):
         seen = set()
-        for i, (iv, where, part, dev) in enumerate(SENDS[n]):
+        for i, (iv, where, part, dev) in enumerate(sends_of(h, n)):
+            if only is not None and iv != only:
+                continue
             if n > 1 and (iv, where) not in seen:
                 seen.add((iv, where))
                 arrived(h, iv, where)
-            kv_hop(h, iv, place(*where), part, devs[dev], first_sem[n] + i).start()
+            kv_hop(h, iv, place(*where), part, devs[dev], first_sem(h, n) + i).start()
 
     loads[2].wait()
     hid = hidden[...]
@@ -393,18 +389,20 @@
         x = kp[:, h * HD : (h + 1) * HD]
         x = x * lax.rsqrt(jnp.mean(x * x, axis=-1, keepdims=True) + 1e-06) * k_gain[...]
         kbuf[h, s] = x.astype(BF16)
+        if h == 0:
+            stage(1, 0, 0)
     vp = jnp.dot(hid, w3[2], preferred_element_type=F32)
     for h in range(heads):
         vbuf[h, s] = jnp.transpose(vp[:, h * HD : (h + 1) * HD]).astype(BF16)
-        if h < 2:
-            stage(1, h)
+        if h == 0:
+            stage(1, 0, 1)
     qp = jnp.dot(hid, w3[0], preferred_element_type=F32)
     for h in range(heads):
         x = qp[:, h * HD : (h + 1) * HD]
         x = x * lax.rsqrt(jnp.mean(x * x, axis=-1, keepdims=True) + 1e-06) * q_gain[...]
         qbuf[h] = jnp.transpose(x).astype(BF16)
     stage(2, 0)
-    stage(1, 2)
+    stage(1, 1)
     stage(3, 0)
 
     w_r1.wait_recv()
@@ -412,36 +410,51 @@
     w_p3 = w_hop(2, 0, NV, partner, 15)
     w_p3.start()
 
-    bias = jnp.where(alive > 0.5, 0.0, -1e30)
+    tail_row = lax.broadcasted_iota(jnp.int32, (HD, nloc), 0)
+    q_tail = jnp.where(tail_row == 0, 1.0, 0.0).astype(BF16)
+    tail_col = lax.broadcasted_iota(jnp.int32, (nloc, HD), 1)
+    k_tail[...] = jnp.where(tail_col == 0, jnp.where(alive > 0.5, 0.0, -1e30), 0.0).astype(BF16)
+    v_tail = jnp.ones((16, nloc), BF16)
     coef = math.log2(math.e) / math.sqrt(HD)
 
     def attend(h, g, carry):
         for dy in range(4):
             for iv in (0, 1):
                 arrived(h, iv, (g, dy, 1))
-        q = qbuf[h]
-
-        def step(j, carry):
-            m, l, acc = carry
-            slot = mod(xl + g, 2) * 8 + lax.rem(y + j // 2, 4) * 2 + lax.rem(core + j, 2)
-            st = jnp.dot(kbuf[h, slot], q, preferred_element_type=F32)
-            st = st * coef + bias
+        q = jnp.concatenate([qbuf[h], q_tail], 0)
+
+        def score(j):
+            jj = lax.rem(j, 8)
+            k = jnp.concatenate([kbuf[h, where(jj)], k_tail[...]], 1)
+            return jnp.dot(k, q, preferred_element_type=F32)
+
+        def where(j):
+            return mod(xl + g, 2) * 8 + lax.rem(y + j // 2, 4) * 2 + lax.rem(core + j, 2)
+
+        def soft(st, j, carry):
+            m, acc = carry
             new = jnp.maximum(m, jnp.max(st, axis=0, keepdims=True))
-            alpha = jnp.exp2(m - new)
-            p = jnp.exp2(st - new)
-            l = l * alpha + jnp.sum(p, axis=0, keepdims=True)
-            acc = acc * alpha + jnp.dot(
-                vbuf[h, slot], p.astype(BF16), preferred_element_type=F32
-            )
-            return new, l, acc
-
-        return lax.fori_loop(0, 8, step, carry)
+            alpha = jnp.exp2((m - new) * coef)
+            p = jnp.exp2((st - new) * coef).astype(BF16)
+            vv = jnp.concatenate([vbuf[h, where(j)], v_tail], 0)
+            return new, acc * alpha + jnp.dot(vv, p, preferred_element_type=F32)
+
+        score_a[...] = score(0)
+
+        def step(i, carry):
+            for u in range(UNROLL):
+                j = UNROLL * i + u
+                now, later = (score_a, score_b) if u % 2 == 0 else (score_b, score_a)
+                later[...] = score(j + 1)
+                carry = soft(now[...], j, carry)
+            return carry
+
+        return lax.fori_loop(0, 8 // UNROLL, step, carry)
 
     def fresh():
         return (
             jnp.full((1, nloc), -1e30, F32),
-            jnp.zeros((1, nloc), F32),
-            jnp.zeros((HD, nloc), F32),
+            jnp.zeros((HD + 16, nloc), F32),
         )
 
     og = []
@@ -456,39 +469,42 @@
         )
 
     def finish(h, carry):
-        m, l, acc = carry
-        obuf[v, :, pl.ds(h * HD, HD)] = jnp.transpose(acc / l).astype(BF16)
+        _, acc = carry
+        out = acc[:HD] / acc[HD : HD + 1]
+        obuf[v, :, pl.ds(h * HD, HD)] = jnp.transpose(out).astype(BF16)
 
     c = attend(0, 0, fresh())
     stage(2, 1)
     stage(4, 0)
     c = attend(0, 1, c)
-    stage(3, 1)
-    stage(2, 2)
     finish(0, c)
     og[0][0]()
+    stage(1, 2)
+    stage(3, 1)
+    og[0][1]()
     c = attend(1, 0, fresh())
+    stage(2, 2)
     stage(4, 1)
-    stage(3, 2)
-    og[0][1]()
+    og[0][2]()
     c = attend(1, 1, c)
-    og[0][2]()
     finish(1, c)
     og[1][0]()
+    stage(3, 2)
+    og[1][1]()
     c = attend(2, 0, fresh())
+    og[1][2]()
     stage(4, 2)
-    og[1][1]()
     c = attend(2, 1, c)
-    og[1][2]()
     finish(2, c)
     og[2][0]()
     w_pt.wait_recv()
     w_p1.wait_recv()
     w_p2.wait_recv()
     w_p3.wait_recv()
+    og[2][1]()
     og[0][3]()
     og[1][3]()
-    og[2][1]()
+    og[2][2]()
 
     def project(lo, n, start):
         def add(u, acc):
@@ -499,7 +515,6 @@
         return lax.fori_loop(0, NV, add, start)
 
     mixed = project(0, 2 * HD, jnp.zeros((nloc, cols), F32))
-    og[2][2]()
     og[2][3]()
     mixed = project(2 * HD, HD, mixed)
     here = pl.ds(pl.multiple_of(v * cols, 128), cols)
@@ -509,8 +524,8 @@
     for h in range(heads):
         og[h][4]()
         for n in (1, 2, 3, 4):
-            for i, (iv, where, part, dev) in enumerate(SENDS[n]):
-                kv_hop(h, iv, place(*where), part, devs[dev], first_sem[n] + i).wait_send()
+            for i, (iv, where, part, dev) in enumerate(sends_of(h, n)):
+                kv_hop(h, iv, place(*where), part, devs[dev], first_sem(h, n) + i).wait_send()
     for c in (w_up, w_dn, w_pt, w_r1, w_p1, w_r2, w_p2, w_p3):
         c.wait_send()
 
@@ -554,6 +569,9 @@
             pltpu.VMEM((heads, HD, nloc), BF16),
             pltpu.VMEM((NV, nloc, cols), BF16),
             pltpu.VMEM((NV, cols, cols), BF16),
+            pltpu.VMEM((nloc, nloc), F32),
+            pltpu.VMEM((nloc, nloc), F32),
+            pltpu.VMEM((nloc, HD), BF16),
             dma((4,)),
             dma((2,)),
             dma((NV,)),
@@ -564,7 +582,7 @@
             dma((9,)),
             dma((16,)),
             dma((16,)),
-            dma((heads, 33)),
+            dma((heads, 34)),
             dma((heads, NS, 2)),
             dma((heads, NS, 2)),
             dma((heads, 9)),

time: 135 us -> 123 us (0.911)
  Pallas kernels: 133 us -> 120 us
    pallas_call x1, Pallas kernels: 133 us -> 120 us  [body(): pl.pallas_call(fused_kernel, name='fused', out_shape=jax.ShapeDtypeStruct...]
where the time goes in v3:
time: 123 us; the launch traced here: 122 us
  Pallas kernels  120 us (98%)
  local copies, waits for them, and re-layouts  1.78 us (1%)
    pallas_call x1, Pallas kernels, body(): pl.pallas_call(fused_kernel, name='fused', out_shape=jax.ShapeDtypeStruct...  120 us

profile of v3, /device:TPU:0, one launch (start us, length us, event | category | flops | bytes accessed | tf_op | source)
XLA Modules:
  0.0 121.9 jit_solution(7822010576056219157)
XLA Ops:
  0.0 120.1 %fused.1 = bf16[512,384]{1,0:T(8,128)(2,1)} custom-call(f32[64,512]{1,0:T(8,128)} %bitcast.14, s32[8]{0:T(128)} %counts.1, f32[3,512,512]{2,1,0:T(8,128)} %conv_w_hbm.1, f32[1,512]{1,0:T(1,128)} %bitcast.19, f32[1,512]{1,0:T(1,128)} %bitcast.20, f32[1,512]{1,0:T(1,128)} %bitcast.21, bf16[512,3072]{1,0:T(8,128)(2,1)} %embed_w_hbm.1, f32[1,3072]{1,0:T(1,128)} %bitcast.15, ...), custom_call_target="tpu_custom_call" | custom-call | tf_op jit(solution)/shard_map/fused/pallas_call | solution.py:546
  120.1 1.8 %copy.17 = bf16[32,16,384]{2,1,0:T(8,128)(2,1)} copy(bf16[32,16,384]{2,1,0:T(8,128)(2,1)} %bitcast.13) | data formatting | bytes 786432
